TPU v7x, 32 devices: a whole 2x2x4 slice. The times are simulated.
32 devices in a mesh: dp: 16 (over z, y, core), mp: 2 (over x).
Axes of the slice: x: 2, y: 2, z: 4, core: 2. Of those that a mesh axis runs over, the one named last changes fastest.
Arguments:
- tokens_in: bfloat16 [4096, 2048], P(('dp', 'mp')), may hold values from -6 to 6
- teacher: bfloat16 [4096, 2048], P(('dp', 'mp')), may hold values from -6 to 6
- valid_mask: int32 [16, 256], P('dp', 'mp'), may hold values from 0 to 1, as said below
- group_of: int32 [16], replicated, may hold values from 0 to 1, as said below
- prompt_len: int32 [2], replicated, may hold values from 128 to 256
- ln1_gain: bfloat16 [2048], P('dp'), may hold values from 0.5 to 1.5
- ln1_bias: bfloat16 [2048], P('dp'), may hold values from -2 to 2
- w_query: bfloat16 [2048, 2048], P('dp', 'mp'), may hold values from -0.125 to 0.125
- w_key: bfloat16 [2048, 2048], P('dp', 'mp'), may hold values from -0.125 to 0.125
- w_value: bfloat16 [2048, 4096], P('dp', 'mp'), may hold values from -0.125 to 0.125
- w_gate: bfloat16 [2048, 4096], P('dp', 'mp'), may hold values from -0.125 to 0.125
- w_out: bfloat16 [2048, 4096], P('dp', 'mp'), may hold values from -0.1875 to 0.1875
- ln2_gain: bfloat16 [2048], P('dp'), may hold values from 0.5 to 1.5
- ln2_bias: bfloat16 [2048], P('dp'), may hold values from -2 to 2
- w_up: bfloat16 [2048, 4096], P('dp', 'mp'), may hold values from -0.125 to 0.125
- w_down: bfloat16 [2048, 4096], P('dp', 'mp'), may hold values from -0.125 to 0.125
Outputs:
- block_out: float32 [4096, 2048], P(('dp', 'mp'))
- grad_tokens: float32 [4096, 2048], P(('dp', 'mp'))
- loss: float32 [], replicated
- grad_ln1_gain: float32 [2048], P('dp')
- grad_ln1_bias: float32 [2048], P('dp')
- grad_w_query: float32 [2048, 2048], P('dp', 'mp')
- grad_w_key: float32 [2048, 2048], P('dp', 'mp')
- grad_w_value: float32 [2048, 4096], P('dp', 'mp')
- grad_w_gate: float32 [2048, 4096], P('dp', 'mp')
- grad_w_out: float32 [2048, 4096], P('dp', 'mp')
- grad_ln2_gain: float32 [2048], P('dp')
- grad_ln2_bias: float32 [2048], P('dp')
- grad_w_up: float32 [2048, 4096], P('dp', 'mp')
- grad_w_down: float32 [2048, 4096], P('dp', 'mp')
Inputs may be any that keep to these rules, and one draw needn't show every extreme that they name: `valid_mask`: in each row the ones form a leading run of one or more positions, zeros follow. `group_of`: each group number is held by exactly 8 segments; a group's prompt is its lowest-numbered segment, the others are its continuations.
All inputs are finite; a program needn't handle non-finite values.
Results may differ from a plain program's by a relative error of at most 0.013.
Values may be sent and summed in bfloat16 or wider, within the bound.
A program may use at most 192 MiB of HBM per device.

v0:
```python
import math
import jax
import jax.numpy as jnp
from jax import lax
from jax.sharding import PartitionSpec as P

DK = 256
DV = 512
EPSILON = 1e-05
GROUP_EPSILON = 0.05


def norm_stats(values, floor_eps):
    center = jnp.mean(values, axis=-1, keepdims=True)
    shifted = values - center
    inv_std = lax.rsqrt(jnp.mean(shifted * shifted, axis=-1, keepdims=True) + floor_eps)
    return (shifted * inv_std, inv_std)


def norm_back(grad_in, normed, inv_std):
    mean_grad = jnp.mean(grad_in, axis=-1, keepdims=True)
    mean_proj = jnp.mean(grad_in * normed, axis=-1, keepdims=True)
    return (grad_in - mean_grad - normed * mean_proj) * inv_std


def xpos_tables(positions, direction):
    half_dim = DK // 2
    pair_index = jnp.arange(half_dim, dtype=jnp.float32)
    frequency = jnp.exp(-(2.0 * pair_index / DK) * math.log(10000.0))
    base_ratio = (2.0 * pair_index / DK + 0.4) / 1.4
    angles = positions[:, None] * frequency[None, :]
    factor = jnp.exp(direction * (positions[:, None] / 512.0) * jnp.log(base_ratio)[None, :])
    return (jnp.cos(angles), jnp.sin(angles), factor)


def rotate_pairs(values, cosine, sine_tab, factor):
    half_dim = values.shape[-1] // 2
    first_half = values[..., :half_dim]
    second = values[..., half_dim:]
    cosine = cosine[:, None, :]
    sine_tab = sine_tab[:, None, :]
    factor = factor[:, None, :]
    return jnp.concatenate(
        [
            (first_half * cosine - second * sine_tab) * factor,
            (second * cosine + first_half * sine_tab) * factor,
        ],
        axis=-1,
    )


def rotate_back(grad_rot, cosine, sine_tab, factor):
    half_dim = grad_rot.shape[-1] // 2
    first_half = grad_rot[..., :half_dim]
    second = grad_rot[..., half_dim:]
    cosine = cosine[:, None, :]
    sine_tab = sine_tab[:, None, :]
    factor = factor[:, None, :]
    return jnp.concatenate(
        [
            (first_half * cosine + second * sine_tab) * factor,
            (second * cosine - first_half * sine_tab) * factor,
        ],
        axis=-1,
    )


def plain_dot(first_op, second_op):
    return jnp.dot(first_op, second_op, preferred_element_type=jnp.float32)


def contract_last(first_op, second_op):
    return lax.dot_general(
        first_op, second_op, (((1,), (1,)), ((), ())), preferred_element_type=jnp.float32
    )


def contract_first(first_op, second_op):
    return lax.dot_general(
        first_op, second_op, (((0,), (0,)), ((), ())), preferred_element_type=jnp.float32
    )


def gather_rows(rows_low):
    return lax.all_gather(rows_low, "mp", axis=0, tiled=True)


def scatter_rows(terms):
    return lax.psum_scatter(terms, "mp", scatter_dimension=0, tiled=True)


def on_device(
    tokens_in,
    teacher,
    valid_mask,
    group_of,
    prompt_len,
    ln1_gain,
    ln1_bias,
    w_query,
    w_key,
    w_value,
    w_gate,
    w_out,
    ln2_gain,
    ln2_bias,
    w_up,
    w_down,
):
    half_rows = tokens_in.shape[0]
    model_dim = tokens_in.shape[1]
    seg_len = half_rows * lax.axis_size("mp")
    seg_count = group_of.shape[0]
    group_count = prompt_len.shape[0]
    heads_local = w_query.shape[1] // DK
    token_total = seg_len * seg_count
    dp_index = lax.axis_index("dp")
    mp_index = lax.axis_index("mp")
    attn_full = (
        lax.all_gather(ln1_gain, "dp", axis=0, tiled=True),
        lax.all_gather(ln1_bias, "dp", axis=0, tiled=True),
        lax.all_gather(w_query, "dp", axis=0, tiled=True),
        lax.all_gather(w_key, "dp", axis=0, tiled=True),
        lax.all_gather(w_value, "dp", axis=0, tiled=True),
        lax.all_gather(w_gate, "dp", axis=0, tiled=True),
        lax.all_gather(w_out, "dp", axis=0, tiled=True),
    )
    ffn_full = (
        lax.all_gather(ln2_gain, "dp", axis=0, tiled=True),
        lax.all_gather(ln2_bias, "dp", axis=0, tiled=True),
        lax.all_gather(w_up, "dp", axis=0, tiled=True),
        lax.all_gather(w_down, "dp", axis=0, tiled=True),
    )
    gain_one = attn_full[0].astype(jnp.float32)
    bias_one = attn_full[1].astype(jnp.float32)
    wq_full, wk_full, wv_full, wg_full, wo_full = (
        attn_full[2],
        attn_full[3],
        attn_full[4],
        attn_full[5],
        attn_full[6],
    )
    gain_two = ffn_full[0].astype(jnp.float32)
    bias_two = ffn_full[1].astype(jnp.float32)
    wu_full, wd_full = (ffn_full[2], ffn_full[3])
    segment_ids = jnp.arange(seg_count, dtype=jnp.int32)
    my_group = jnp.sum(jnp.where(segment_ids == dp_index, group_of, 0))
    first_member = jnp.min(jnp.where(group_of == my_group, segment_ids, seg_count))
    prompt_flag = (first_member == dp_index).astype(jnp.float32)
    group_match = jnp.arange(group_count, dtype=jnp.int32) == my_group
    group_onehot = group_match.astype(jnp.float32)
    prompt_size = jnp.sum(jnp.where(group_match, prompt_len, 0))
    token_ids = jnp.arange(seg_len, dtype=jnp.int32)
    offset = jnp.where(prompt_flag > 0, 0, prompt_size)
    positions = (token_ids + offset).astype(jnp.float32)
    head_ids = (mp_index * heads_local + jnp.arange(heads_local, dtype=jnp.int32)).astype(
        jnp.float32
    )
    log_decay = jnp.log(1.0 - 2.0 ** (-5.0 - head_ids))
    before_end = token_ids < prompt_size
    state_age = (prompt_size - 1 - token_ids).astype(jnp.float32)
    state_weighting = jnp.where(
        (before_end & (prompt_flag > 0))[:, None],
        jnp.exp(log_decay[None, :] * jnp.maximum(state_age, 0.0)[:, None]),
        0.0,
    )
    continuation_factor = (1.0 - prompt_flag) * jnp.exp(
        log_decay[None, :] * (token_ids.astype(jnp.float32) + 1.0)[:, None]
    )
    float_ids = token_ids.astype(jnp.float32)
    distance = float_ids[:, None] - float_ids[None, :]
    decay_mat = jnp.where(
        distance[None] >= 0.0,
        jnp.exp(log_decay[:, None, None] * jnp.maximum(distance, 0.0)[None]),
        0.0,
    )
    own_ids = mp_index * half_rows + jnp.arange(half_rows, dtype=jnp.int32)
    loss_mask = valid_mask[0].astype(jnp.float32) * jnp.where(
        prompt_flag > 0, own_ids < prompt_size, True
    ).astype(jnp.float32)
    token_rows = tokens_in.astype(jnp.float32)
    normed_one, inv_one = norm_stats(token_rows, EPSILON)
    a_all = gather_rows((normed_one * gain_one + bias_one).astype(jnp.bfloat16))
    queries = plain_dot(a_all, wq_full).reshape(seg_len, heads_local, DK)
    keys_raw = plain_dot(a_all, wk_full).reshape(seg_len, heads_local, DK)
    reduced_values = (
        plain_dot(a_all, wv_full).astype(jnp.bfloat16).reshape(seg_len, heads_local, DV)
    )
    gate_pre = plain_dot(a_all, wg_full)
    cosine, sine_tab, grow_fac = xpos_tables(positions, 1.0)
    _, _, shrink = xpos_tables(positions, -1.0)
    q_scale = DK ** (-0.5)
    rotated_queries = (rotate_pairs(queries, cosine, sine_tab, grow_fac) * q_scale).astype(
        jnp.bfloat16
    )
    rotated_keys = rotate_pairs(keys_raw, cosine, sine_tab, shrink).astype(jnp.bfloat16)
    local_state = jnp.einsum(
        "jld,jla->lda",
        rotated_keys.astype(jnp.float32) * state_weighting[:, :, None],
        reduced_values.astype(jnp.float32),
        precision=lax.Precision.HIGHEST,
    )
    slots = group_onehot[:, None, None, None] * (prompt_flag * local_state)[None]
    summed = lax.psum(slots, "dp")
    state_lookup = jnp.sum(summed * group_onehot[:, None, None, None], axis=0).astype(jnp.bfloat16)
    scores = jnp.einsum(
        "thk,nhk->htn", rotated_queries, rotated_keys, preferred_element_type=jnp.float32
    )
    weights_low = (scores * decay_mat).astype(jnp.bfloat16)
    retained_output = jnp.einsum(
        "htn,nhv->thv", weights_low, reduced_values, preferred_element_type=jnp.float32
    )
    carried_forward = jnp.einsum(
        "ozi,ziw->ozw", rotated_queries, state_lookup, preferred_element_type=jnp.float32
    )
    retained_output = retained_output + continuation_factor[:, :, None] * carried_forward
    grouped, inv_group = norm_stats(retained_output, GROUP_EPSILON)
    gate_act = jax.nn.silu(gate_pre).reshape(seg_len, heads_local, DV)
    gated_out = (gate_act * grouped).reshape(seg_len, heads_local * DV).astype(jnp.bfloat16)
    attn_own = scatter_rows(contract_last(gated_out, wo_full))
    hidden_res = token_rows + attn_own
    normed_two, inv_two = norm_stats(hidden_res, EPSILON)
    c_all = gather_rows((normed_two * gain_two + bias_two).astype(jnp.bfloat16))
    up_pre = plain_dot(c_all, wu_full)
    up_act = jax.nn.gelu(up_pre, approximate=False).astype(jnp.bfloat16)
    ffn_own = scatter_rows(contract_last(up_act, wd_full))
    block_out = hidden_res + ffn_own
    error_rows = block_out - teacher.astype(jnp.float32)
    weighted = loss_mask[:, None] * error_rows
    valid_count, squared = lax.psum(
        (jnp.sum(loss_mask), jnp.sum(weighted * error_rows)), ("dp", "mp")
    )
    grad_out = token_total / valid_count * weighted
    loss_value = squared / (valid_count * model_dim)
    grad_ffn_all = gather_rows(grad_out.astype(jnp.bfloat16))
    grad_up_act = plain_dot(grad_ffn_all, wd_full)
    _, gelu_pull = jax.vjp(lambda inner: jax.nn.gelu(inner, approximate=False), up_pre)
    grad_up = gelu_pull(grad_up_act)[0].astype(jnp.bfloat16)
    grad_wd = contract_first(grad_ffn_all, up_act)
    grad_wu = contract_first(c_all, grad_up)
    grad_c = scatter_rows(contract_last(grad_up, wu_full))
    grad_gain2_part = jnp.sum(grad_c * normed_two, axis=0)
    grad_bias2_part = jnp.sum(grad_c, axis=0)
    grad_hidden = grad_out + norm_back(grad_c * gain_two, normed_two, inv_two)
    ffn_reduced = (
        lax.psum_scatter(grad_gain2_part, "dp", scatter_dimension=0, tiled=True),
        lax.psum_scatter(grad_bias2_part, "dp", scatter_dimension=0, tiled=True),
        lax.psum_scatter(grad_wu, "dp", scatter_dimension=0, tiled=True),
        lax.psum_scatter(grad_wd, "dp", scatter_dimension=0, tiled=True),
    )
    grad_attn_all = gather_rows(grad_hidden.astype(jnp.bfloat16))
    grad_gated = plain_dot(grad_attn_all, wo_full).reshape(seg_len, heads_local, DV)
    grad_wo = contract_first(grad_attn_all, gated_out)
    _, silu_pull = jax.vjp(jax.nn.silu, gate_pre)
    grad_gate = silu_pull((grad_gated * grouped).reshape(seg_len, heads_local * DV))[0].astype(
        jnp.bfloat16
    )
    retained_gradient = norm_back(grad_gated * gate_act, grouped, inv_group).astype(jnp.bfloat16)
    grad_weights = jnp.einsum(
        "thv,nhv->htn", retained_gradient, reduced_values, preferred_element_type=jnp.float32
    )
    grad_values = jnp.einsum(
        "htn,thv->nhv", weights_low, retained_gradient, preferred_element_type=jnp.float32
    )
    grad_scores = (grad_weights * decay_mat).astype(jnp.bfloat16)
    grad_q_rot = jnp.einsum(
        "htn,nhk->thk", grad_scores, rotated_keys, preferred_element_type=jnp.float32
    )
    grad_q_rot = grad_q_rot + continuation_factor[:, :, None] * jnp.einsum(
        "mjr,jwr->mjw", retained_gradient, state_lookup, preferred_element_type=jnp.float32
    )
    grad_k_rot = jnp.einsum(
        "htn,thk->nhk", grad_scores, rotated_queries, preferred_element_type=jnp.float32
    )
    state_grad_own = jnp.einsum(
        "ybn,ybw->bnw",
        rotated_queries.astype(jnp.float32) * continuation_factor[:, :, None],
        retained_gradient.astype(jnp.float32),
        precision=lax.Precision.HIGHEST,
    )
    grad_slots = group_onehot[:, None, None, None] * state_grad_own[None]
    grad_summed = lax.psum(grad_slots, "dp")
    state_gradient = (
        prompt_flag * jnp.sum(grad_summed * group_onehot[:, None, None, None], axis=0)
    ).astype(jnp.bfloat16)
    grad_k_rot = grad_k_rot + state_weighting[:, :, None] * jnp.einsum(
        "ilm,lpm->ilp", reduced_values, state_gradient, preferred_element_type=jnp.float32
    )
    grad_values = grad_values + state_weighting[:, :, None] * jnp.einsum(
        "zdo,doi->zdi", rotated_keys, state_gradient, preferred_element_type=jnp.float32
    )
    grad_queries = (
        rotate_back(grad_q_rot * q_scale, cosine, sine_tab, grow_fac)
        .reshape(seg_len, heads_local * DK)
        .astype(jnp.bfloat16)
    )
    grad_keys = (
        rotate_back(grad_k_rot, cosine, sine_tab, shrink)
        .reshape(seg_len, heads_local * DK)
        .astype(jnp.bfloat16)
    )
    grad_vlow = grad_values.reshape(seg_len, heads_local * DV).astype(jnp.bfloat16)
    grad_wq = contract_first(a_all, grad_queries)
    grad_wk = contract_first(a_all, grad_keys)
    grad_wv = contract_first(a_all, grad_vlow)
    grad_wg = contract_first(a_all, grad_gate)
    grad_a_terms = (
        contract_last(grad_queries, wq_full)
        + contract_last(grad_keys, wk_full)
        + contract_last(grad_vlow, wv_full)
        + contract_last(grad_gate, wg_full)
    )
    grad_a = scatter_rows(grad_a_terms)
    grad_gain1_part = jnp.sum(grad_a * normed_one, axis=0)
    grad_bias1_part = jnp.sum(grad_a, axis=0)
    grad_tokens = grad_hidden + norm_back(grad_a * gain_one, normed_one, inv_one)
    attn_reduced = (
        lax.psum_scatter(grad_gain1_part, "dp", scatter_dimension=0, tiled=True),
        lax.psum_scatter(grad_bias1_part, "dp", scatter_dimension=0, tiled=True),
        lax.psum_scatter(grad_wq, "dp", scatter_dimension=0, tiled=True),
        lax.psum_scatter(grad_wk, "dp", scatter_dimension=0, tiled=True),
        lax.psum_scatter(grad_wv, "dp", scatter_dimension=0, tiled=True),
        lax.psum_scatter(grad_wg, "dp", scatter_dimension=0, tiled=True),
        lax.psum_scatter(grad_wo, "dp", scatter_dimension=0, tiled=True),
    )
    norm_sums = lax.psum((attn_reduced[0], attn_reduced[1], ffn_reduced[0], ffn_reduced[1]), "mp")
    return (
        block_out,
        grad_tokens,
        loss_value,
        norm_sums[0],
        norm_sums[1],
        attn_reduced[2],
        attn_reduced[3],
        attn_reduced[4],
        attn_reduced[5],
        attn_reduced[6],
        norm_sums[2],
        norm_sums[3],
        ffn_reduced[2],
        ffn_reduced[3],
    )


def solution(mesh):
    return jax.shard_map(
        on_device,
        mesh=mesh,
        in_specs=(
            P(("dp", "mp"), None),
            P(("dp", "mp"), None),
            P("dp", "mp"),
            P(),
            P(),
            P("dp"),
            P("dp"),
            P("dp", "mp"),
            P("dp", "mp"),
            P("dp", "mp"),
            P("dp", "mp"),
            P("dp", "mp"),
            P("dp"),
            P("dp"),
            P("dp", "mp"),
            P("dp", "mp"),
        ),
        out_specs=(
            P(("dp", "mp"), None),
            P(("dp", "mp"), None),
            P(),
            P("dp"),
            P("dp"),
            P("dp", "mp"),
            P("dp", "mp"),
            P("dp", "mp"),
            P("dp", "mp"),
            P("dp", "mp"),
            P("dp"),
            P("dp"),
            P("dp", "mp"),
            P("dp", "mp"),
        ),
        check_vma=False,
    )
```

profile of v0, /device:TPU:0, one launch (start us, length us, event | category | flops | bytes accessed | tf_op | source)
XLA Modules:
  0.0 2218.7 jit_solution(17705684298100000474)
XLA Ops:
  9.8 23.3 %all-gather = bf16[16,1,128]{2,1,0:T(2,128)(2,1)S(1)} all-gather(bf16[1,1,128]{2,1,0:T(2,128)(2,1)} %bitcast.140), channel_id=1, replica_groups=mesh['dp'=16,'mp'=2] {'dp'}, dimensions={0}, use_global_device_ids=true | all-gather | bytes 4352 | tf_op jit(solution)/shard_map/all_gather | solution.py:120
  72.8 52.6 %all-gather.24.cloned.1.call-done = bf16[2048,1024]{1,0:T(8,128)(2,1)} async-done(((bf16[128,1024]{1,0:T(8,128)(2,1)}), bf16[2048,1024]{1,0:T(8,128)(2,1)}) %all-gather.24.cloned.1.call-update) | async-done | bytes 4194320 | tf_op jit(solution)/shard_map/all_gather | solution.py:123
  129.7 46.8 %all-gather.22.cloned.1.call-done = bf16[2048,1024]{1,0:T(8,128)(2,1)} async-done(((bf16[128,1024]{1,0:T(8,128)(2,1)}), bf16[2048,1024]{1,0:T(8,128)(2,1)}) %all-gather.22.cloned.1.call-update) | async-done | bytes 4194320 | tf_op jit(solution)/shard_map/all_gather | solution.py:122
  185.0 66.4 %all-gather.20.cloned.1.call-done = bf16[2048,2048]{1,0:T(8,128)(2,1)} async-done(((bf16[128,2048]{1,0:T(8,128)(2,1)}), bf16[2048,2048]{1,0:T(8,128)(2,1)}) %all-gather.20.cloned.1.call-update) | async-done | bytes 8388624 | tf_op jit(solution)/shard_map/all_gather | solution.py:124
  265.3 61.1 %all-gather.18.cloned.1.call-done = bf16[2048,2048]{1,0:T(8,128)(2,1)} async-done(((bf16[128,2048]{1,0:T(8,128)(2,1)}), bf16[2048,2048]{1,0:T(8,128)(2,1)}) %all-gather.18.cloned.1.call-update) | async-done | bytes 8388624 | tf_op jit(solution)/shard_map/all_gather | solution.py:125
  339.0 100.7 %all-reduce.10.cloned.1.call-done = f32[2,4,256,512]{3,2,1,0:T(8,128)} async-done(((f32[2,4,256,512]{3,2,1,0:T(8,128)}), f32[2,4,256,512]{3,2,1,0:T(8,128)}) %all-reduce.10.cloned.1.call-update) | async-done | bytes 4194320 | tf_op jit(solution)/shard_map/psum | solution.py:204
  445.8 69.5 %all-gather.26.cloned.1.call-done = bf16[2048,2048]{1,0:T(8,128)(2,1)} async-done(((bf16[128,2048]{1,0:T(8,128)(2,1)}), bf16[2048,2048]{1,0:T(8,128)(2,1)}) %all-gather.26.cloned.1.call-update) | async-done | bytes 8388624 | tf_op jit(solution)/shard_map/all_gather | solution.py:126
  523.2 19.0 all-gather.2
  564.7 64.9 %all-gather.30.cloned.1.call-done = bf16[2048,2048]{1,0:T(8,128)(2,1)} async-done(((bf16[128,2048]{1,0:T(8,128)(2,1)}), bf16[2048,2048]{1,0:T(8,128)(2,1)}) %all-gather.30.cloned.1.call-update) | async-done | bytes 8388624 | tf_op jit(solution)/shard_map/all_gather | solution.py:131
  629.6 21.9 all-gather.28.cloned.1.call-done
  662.1 65.9 %all-gather.32.cloned.1.call-done = bf16[2048,2048]{1,0:T(8,128)(2,1)} async-done(((bf16[128,2048]{1,0:T(8,128)(2,1)}), bf16[2048,2048]{1,0:T(8,128)(2,1)}) %all-gather.32.cloned.1.call-update) | async-done | bytes 8388624 | tf_op jit(solution)/shard_map/all_gather | solution.py:132
  737.8 28.2 %reduce-scatter.14.cloned.1.call-done = f32[128,2048]{1,0:T(8,128)} async-done(((f32[256,2048]{1,0:T(8,128)}), f32[128,2048]{1,0:T(8,128)}) %reduce-scatter.14.cloned.1.call-update) | async-done | bytes 1048592 | tf_op jit(solution)/shard_map/reduce_scatter | solution.py:89
  769.2 39.5 %all-reduce.4 = (f32[]{:T(128)}, f32[]{:T(128)}) all-reduce(f32[]{:T(128)} %get-tuple-element.39, f32[]{:T(128)} %get-tuple-element.37), channel_id=1, replica_groups=mesh['dp'=16,'mp'=2] {'dp','mp'}, use_global_device_ids=true, to_apply=%region_14.15 | all-reduce | flops 2 | bytes 16 | tf_op jit(solution)/shard_map/psum | solution.py:230
  811.9 22.3 %all-gather.34.cloned.1.call-done = bf16[256,2048]{1,0:T(8,128)(2,1)} async-done(((bf16[128,2048]{1,0:T(8,128)(2,1)}), bf16[256,2048]{1,0:T(8,128)(2,1)}) %all-gather.34.cloned.1.call-update) | async-done | bytes 1048592 | tf_op jit(solution)/shard_map/all_gather | solution.py:85
  850.2 31.8 %reduce-scatter.16.cloned.1.call-done = f32[128,2048]{1,0:T(8,128)} async-done(((f32[256,2048]{1,0:T(8,128)}), f32[128,2048]{1,0:T(8,128)}) %reduce-scatter.16.cloned.1.call-update) | async-done | bytes 1048592 | tf_op jit(solution)/shard_map/reduce_scatter | solution.py:89
  887.6 21.4 all-gather.36.cloned.1.call-done
  936.8 98.4 %all-reduce.12.cloned.1.call-done = f32[2,4,256,512]{3,2,1,0:T(8,128)} async-done(((f32[2,4,256,512]{3,2,1,0:T(8,128)}), f32[2,4,256,512]{3,2,1,0:T(8,128)}) %all-reduce.12.cloned.1.call-update) | async-done | bytes 4194320 | tf_op jit(solution)/shard_map/psum | solution.py:282
  1124.5 62.8 %all-reduce.5 = (f32[2048]{0:T(1024)S(1)}, f32[2048]{0:T(1024)S(1)}, f32[2048]{0:T(1024)S(1)}, f32[2048]{0:T(1024)S(1)}) all-reduce(f32[2048]{0:T(1024)S(1)} %get-tuple-element.18, f32[2048]{0:T(1024)S(1)} %get-tuple-element.23, f32[2048]{0:T(1024)S(1)} %copy-done.51, ...), channel_id=6, replica_groups=mesh['dp'=16,'mp'=2] {'dp'}, use_global_device_ids=true, to_apply=%region_28.29.clone | all-reduce | flops 8192 | bytes 65536
  1196.8 107.8 %reduce-scatter.20.cloned.1.call-done = f32[128,1024]{1,0:T(8,128)} async-done(((f32[2048,1024]{1,0:T(8,128)}), f32[128,1024]{1,0:T(8,128)}) %reduce-scatter.20.cloned.1.call-update) | async-done | bytes 524304 | tf_op jit(solution)/shard_map/reduce_scatter | solution.py:320
  1304.6 181.5 %reduce-scatter.30.cloned.1.call-done = f32[128,2048]{1,0:T(8,128)} async-done(((f32[2048,2048]{1,0:T(8,128)}), f32[128,2048]{1,0:T(8,128)}) %reduce-scatter.30.cloned.1.call-update) | async-done | bytes 1048592 | tf_op jit(solution)/shard_map/reduce_scatter | solution.py:248
  1486.1 181.1 %reduce-scatter.32.cloned.1.call-done = f32[128,2048]{1,0:T(8,128)} async-done(((f32[2048,2048]{1,0:T(8,128)}), f32[128,2048]{1,0:T(8,128)}) %reduce-scatter.32.cloned.1.call-update) | async-done | bytes 1048592 | tf_op jit(solution)/shard_map/reduce_scatter | solution.py:249
  1667.3 181.1 %reduce-scatter.28.cloned.1.call-done = f32[128,2048]{1,0:T(8,128)} async-done(((f32[2048,2048]{1,0:T(8,128)}), f32[128,2048]{1,0:T(8,128)}) %reduce-scatter.28.cloned.1.call-update) | async-done | bytes 1048592 | tf_op jit(solution)/shard_map/reduce_scatter | solution.py:324
  1848.4 181.1 %reduce-scatter.26.cloned.1.call-done = f32[128,2048]{1,0:T(8,128)} async-done(((f32[2048,2048]{1,0:T(8,128)}), f32[128,2048]{1,0:T(8,128)}) %reduce-scatter.26.cloned.1.call-update) | async-done | bytes 1048592 | tf_op jit(solution)/shard_map/reduce_scatter | solution.py:323
  2029.5 181.0 %reduce-scatter.24.cloned.1.call-done = f32[128,2048]{1,0:T(8,128)} async-done(((f32[2048,2048]{1,0:T(8,128)}), f32[128,2048]{1,0:T(8,128)}) %reduce-scatter.24.cloned.1.call-update) | async-done | bytes 1048592 | tf_op jit(solution)/shard_map/reduce_scatter | solution.py:322
  (307 shorter events, 287.3 us)
Async XLA Ops:
  7.2 65.6 %all-gather.16.cloned.1.call-start = ((), (), s32[]{:S(2)}) async-start(), calls=%async_computation.11 | async-start | bytes 1572864 | tf_op jit(solution)/shard_map/all_gather | solution.py:85
  53.1 72.4 %all-gather.24.cloned.1.call-start = ((), (), s32[]{:S(2)}) async-start(), calls=%async_computation.15 | async-start | bytes 4456448 | tf_op jit(solution)/shard_map/all_gather | solution.py:123
  53.8 122.7 %all-gather.22.cloned.1.call-start = ((), (), s32[]{:S(2)}) async-start(), calls=%async_computation.14 | async-start | bytes 4456448 | tf_op jit(solution)/shard_map/all_gather | solution.py:122
  54.5 196.9 %all-gather.20.cloned.1.call-start = ((), (), s32[]{:S(2)}) async-start(), calls=%async_computation.13 | async-start | bytes 8912896 | tf_op jit(solution)/shard_map/all_gather | solution.py:124
  55.1 271.2 %all-gather.18.cloned.1.call-start = ((), (), s32[]{:S(2)}) async-start(), calls=%async_computation.12 | async-start | bytes 8912896 | tf_op jit(solution)/shard_map/all_gather | solution.py:125
  55.7 384.0 %all-reduce.10.cloned.1.call-start = ((), (), s32[]{:S(2)}) async-start(), calls=%async_computation.16 | async-start | bytes 8388608 | tf_op jit(solution)/shard_map/psum | solution.py:204
  261.1 254.1 %all-gather.26.cloned.1.call-start = ((), (), s32[]{:S(2)}) async-start(), calls=%async_computation.17 | async-start | bytes 8912896 | tf_op jit(solution)/shard_map/all_gather | solution.py:126
  261.9 298.4 %reduce-scatter.12.cloned.1.call-start = ((), (), s32[]{:S(2)}) async-start(), calls=%async_computation.18 | async-start | bytes 3145728 | tf_op jit(solution)/shard_map/reduce_scatter | solution.py:89
  522.4 107.2 %all-gather.30.cloned.1.call-start = ((), (), s32[]{:S(2)}) async-start(), calls=%async_computation.20 | async-start | bytes 8912896 | tf_op jit(solution)/shard_map/all_gather | solution.py:131
  523.2 128.3 %all-gather.28.cloned.1.call-start = ((), (), s32[]{:S(2)}) async-start(), calls=%async_computation.19 | async-start | bytes 1572864 | tf_op jit(solution)/shard_map/all_gather | solution.py:85
  563.7 164.2 %all-gather.32.cloned.1.call-start = ((), (), s32[]{:S(2)}) async-start(), calls=%async_computation.21 | async-start | bytes 8912896 | tf_op jit(solution)/shard_map/all_gather | solution.py:132
  564.5 201.6 %reduce-scatter.14.cloned.1.call-start = ((), (), s32[]{:S(2)}) async-start(), calls=%async_computation.22 | async-start | bytes 3145728 | tf_op jit(solution)/shard_map/reduce_scatter | solution.py:89
  735.4 98.8 %all-gather.34.cloned.1.call-start = ((), (), s32[]{:S(2)}) async-start(), calls=%async_computation.23 | async-start | bytes 1572864 | tf_op jit(solution)/shard_map/all_gather | solution.py:85
  811.8 70.2 %reduce-scatter.16.cloned.1.call-start = ((), (), s32[]{:S(2)}) async-start(), calls=%async_computation.24 | async-start | bytes 3145728 | tf_op jit(solution)/shard_map/reduce_scatter | solution.py:89
  850.0 59.0 %all-gather.36.cloned.1.call-start = ((), (), s32[]{:S(2)}) async-start(), calls=%async_computation.25 | async-start | bytes 1572864 | tf_op jit(solution)/shard_map/all_gather | solution.py:85
  887.6 147.5 %all-reduce.12.cloned.1.call-start = ((), (), s32[]{:S(2)}) async-start(), calls=%async_computation.26 | async-start | bytes 8388608 | tf_op jit(solution)/shard_map/psum | solution.py:282
  923.8 198.8 %reduce-scatter.18.cloned.1.call-start = ((), (), s32[]{:S(2)}) async-start(), calls=%async_computation.27 | async-start | bytes 3145728 | tf_op jit(solution)/shard_map/reduce_scatter | solution.py:89
  1056.9 139.8 %reduce-scatter.22.cloned.1.call-start = ((), (), s32[]{:S(2)}) async-start(), calls=%async_computation.29 | async-start | bytes 8912896 | tf_op jit(solution)/shard_map/reduce_scatter | solution.py:321
  1063.0 241.6 %reduce-scatter.20.cloned.1.call-start = ((), (), s32[]{:S(2)}) async-start(), calls=%async_computation.28 | async-start | bytes 8912896 | tf_op jit(solution)/shard_map/reduce_scatter | solution.py:320
  1067.7 418.4 %reduce-scatter.30.cloned.1.call-start = ((), (), s32[]{:S(2)}) async-start(), calls=%async_computation.33 | async-start | bytes 17825792 | tf_op jit(solution)/shard_map/reduce_scatter | solution.py:248
  1078.3 589.0 %reduce-scatter.32.cloned.1.call-start = ((), (), s32[]{:S(2)}) async-start(), calls=%async_computation.34 | async-start | bytes 17825792 | tf_op jit(solution)/shard_map/reduce_scatter | solution.py:249
  1088.9 759.5 %reduce-scatter.28.cloned.1.call-start = ((), (), s32[]{:S(2)}) async-start(), calls=%async_computation.32 | async-start | bytes 17825792 | tf_op jit(solution)/shard_map/reduce_scatter | solution.py:324
  1099.9 929.6 %reduce-scatter.26.cloned.1.call-start = ((), (), s32[]{:S(2)}) async-start(), calls=%async_computation.31 | async-start | bytes 17825792 | tf_op jit(solution)/shard_map/reduce_scatter | solution.py:323
  1110.0 1100.5 %reduce-scatter.24.cloned.1.call-start = ((), (), s32[]{:S(2)}) async-start(), calls=%async_computation.30 | async-start | bytes 17825792 | tf_op jit(solution)/shard_map/reduce_scatter | solution.py:322
  (73 other events, 2311.2 us)
Sparse Core Ops, SparseCore 0:
  53.2 19.6 all-gather.15
  75.0 50.3 all-gather.23
  127.6 48.8 all-gather.21
  178.5 72.8 all-gather.19
  253.4 72.8 all-gather.17
  329.9 109.7 all-reduce.9
  441.8 73.4 all-gather.25
  522.5 30.4 reduce-scatter.11
  555.2 74.3 all-gather.29
  631.5 19.8 all-gather.27
  653.6 74.2 all-gather.31
  735.5 30.4 reduce-scatter.13
  812.0 22.1 all-gather.33
  850.1 31.8 reduce-scatter.15
  887.7 21.2 all-gather.35
  924.0 111.1 all-reduce.11
  1057.1 31.0 reduce-scatter.17
  1092.6 104.1 reduce-scatter.21
  1201.4 103.1 reduce-scatter.19
  1309.1 176.9 reduce-scatter.29
  1490.8 176.4 reduce-scatter.31
  1671.9 176.3 reduce-scatter.27
  1853.1 176.3 reduce-scatter.25
  2034.0 176.3 reduce-scatter.23
where the time goes:
time: 2230 us; the launch traced here: 2220 us
  waiting for transfers between devices  1780 us (80%)
  blocking collectives  185 us (8%)
  matrix products  155 us (7%)
  other arithmetic  51.2 us (2%)
  local copies, waits for them, and re-layouts  23 us (1%)
    reduce_scatter x1, waiting for transfers between devices, on_device(): lax.psum_scatter(grad_wu, 'dp', scatter_dimension=0, tiled=True)  182 us
    reduce_scatter x1, waiting for transfers between devices, on_device(): lax.psum_scatter(grad_wd, 'dp', scatter_dimension=0, tiled=True)  181 us
    reduce_scatter x1, waiting for transfers between devices, on_device(): lax.psum_scatter(grad_wg, 'dp', scatter_dimension=0, tiled=True)  181 us
    reduce_scatter x1, waiting for transfers between devices, on_device(): lax.psum_scatter(grad_wo, 'dp', scatter_dimension=0, tiled=True)  181 us
    reduce_scatter x1, waiting for transfers between devices, on_device(): lax.psum_scatter(grad_wv, 'dp', scatter_dimension=0, tiled=True)  181 us
    reduce_scatter x1, waiting for transfers between devices, on_device(): lax.psum_scatter(grad_wq, 'dp', scatter_dimension=0, tiled=True)  108 us
    psum x1, waiting for transfers between devices, on_device(): summed = lax.psum(slots, 'dp')  101 us
    psum x1, waiting for transfers between devices, on_device(): grad_summed = lax.psum(grad_slots, 'dp')  98.4 us
  transfers between devices with their start and end apart: 24, of which 22 were waited for; matrix products, arithmetic and copies ran while one was open for 6% of the time, Pallas kernels for 0%

commit v1 on v0

--- a/solution.py
+++ b/solution.py
@@ -1,13 +1,23 @@
+import functools
 import math
 import jax
 import jax.numpy as jnp
 from jax import lax
 from jax.sharding import PartitionSpec as P
+from jax.lax import all_gather
 
 DK = 256
 DV = 512
 EPSILON = 1e-05
 GROUP_EPSILON = 0.05
+
+
+def enter_notes(panel, mesh_name):
+    part_now = all_gather(panel, mesh_name)
+    return jnp.sum(part_now, axis=0)
+
+
+prepare_packet = functools.partial(enter_notes, mesh_name="dp")
 
 
 def norm_stats(values, floor_eps):
@@ -279,7 +289,7 @@
         precision=lax.Precision.HIGHEST,
     )
     grad_slots = group_onehot[:, None, None, None] * state_grad_own[None]
-    grad_summed = lax.psum(grad_slots, "dp")
+    grad_summed = prepare_packet(grad_slots)
     state_gradient = (
         prompt_flag * jnp.sum(grad_summed * group_onehot[:, None, None, None], axis=0)
     ).astype(jnp.bfloat16)

time: 2230 us -> 2470 us (1.11)
  waiting for transfers between devices: 1780 us -> 1990 us
    all_gather x0 -> x1, waiting for transfers between devices: none -> 314 us  [enter_notes(): part_now = all_gather(panel, mesh_name)]
    reduce_scatter x1, waiting for transfers between devices: 182 us -> 71.9 us  [on_device(): lax.psum_scatter(grad_wu, 'dp', scatter_dimension=0, tiled=True)]
    reduce_scatter x1, waiting for transfers between devices: 2.26 us -> 107 us  [on_device(): lax.psum_scatter(grad_wk, 'dp', scatter_dimension=0, tiled=True)]
    psum x1 -> x0, waiting for transfers between devices: 98.4 us -> none  [on_device(): grad_summed = lax.psum(grad_slots, 'dp')]
where the time goes in v1:
time: 2470 us; the launch traced here: 2460 us
  waiting for transfers between devices  1990 us (81%)
  blocking collectives  188 us (8%)
  matrix products  159 us (6%)
  other arithmetic  74 us (3%)
    all_gather x1, waiting for transfers between devices, enter_notes(): part_now = all_gather(panel, mesh_name)  314 us
    reduce_scatter x1, waiting for transfers between devices, on_device(): lax.psum_scatter(grad_wv, 'dp', scatter_dimension=0, tiled=True)  182 us
    reduce_scatter x1, waiting for transfers between devices, on_device(): lax.psum_scatter(grad_wd, 'dp', scatter_dimension=0, tiled=True)  181 us
    reduce_scatter x1, waiting for transfers between devices, on_device(): lax.psum_scatter(grad_wg, 'dp', scatter_dimension=0, tiled=True)  181 us
    reduce_scatter x1, waiting for transfers between devices, on_device(): lax.psum_scatter(grad_wo, 'dp', scatter_dimension=0, tiled=True)  181 us
    reduce_scatter x1, waiting for transfers between devices, on_device(): lax.psum_scatter(grad_wq, 'dp', scatter_dimension=0, tiled=True)  108 us
    reduce_scatter x1, waiting for transfers between devices, on_device(): lax.psum_scatter(grad_wk, 'dp', scatter_dimension=0, tiled=True)  107 us
    psum x1, waiting for transfers between devices, on_device(): summed = lax.psum(slots, 'dp')  101 us
  transfers between devices with their start and end apart: 24, of which 22 were waited for; matrix products, arithmetic and copies ran while one was open for 6% of the time, Pallas kernels for 0%

profile of v1, /device:TPU:0, one launch (start us, length us, event | category | flops | bytes accessed | tf_op | source)
XLA Modules:
  0.0 2458.4 jit_solution(11405579621670392804)
XLA Ops:
  9.8 23.3 all-gather
  72.8 52.6 %all-gather.25.cloned.1.call-done = bf16[2048,1024]{1,0:T(8,128)(2,1)} async-done(((bf16[128,1024]{1,0:T(8,128)(2,1)}), bf16[2048,1024]{1,0:T(8,128)(2,1)}) %all-gather.25.cloned.1.call-update) | async-done | bytes 4194320 | tf_op jit(solution)/shard_map/all_gather | solution.py:133
  129.7 46.8 %all-gather.23.cloned.1.call-done = bf16[2048,1024]{1,0:T(8,128)(2,1)} async-done(((bf16[128,1024]{1,0:T(8,128)(2,1)}), bf16[2048,1024]{1,0:T(8,128)(2,1)}) %all-gather.23.cloned.1.call-update) | async-done | bytes 4194320 | tf_op jit(solution)/shard_map/all_gather | solution.py:132
  185.0 66.4 %all-gather.21.cloned.1.call-done = bf16[2048,2048]{1,0:T(8,128)(2,1)} async-done(((bf16[128,2048]{1,0:T(8,128)(2,1)}), bf16[2048,2048]{1,0:T(8,128)(2,1)}) %all-gather.21.cloned.1.call-update) | async-done | bytes 8388624 | tf_op jit(solution)/shard_map/all_gather | solution.py:134
  265.0 61.3 %all-gather.19.cloned.1.call-done = bf16[2048,2048]{1,0:T(8,128)(2,1)} async-done(((bf16[128,2048]{1,0:T(8,128)(2,1)}), bf16[2048,2048]{1,0:T(8,128)(2,1)}) %all-gather.19.cloned.1.call-update) | async-done | bytes 8388624 | tf_op jit(solution)/shard_map/all_gather | solution.py:135
  339.1 100.5 %all-reduce.9.cloned.1.call-done = f32[2,4,256,512]{3,2,1,0:T(8,128)} async-done(((f32[2,4,256,512]{3,2,1,0:T(8,128)}), f32[2,4,256,512]{3,2,1,0:T(8,128)}) %all-reduce.9.cloned.1.call-update) | async-done | bytes 4194320 | tf_op jit(solution)/shard_map/psum | solution.py:214
  445.8 69.5 %all-gather.27.cloned.1.call-done = bf16[2048,2048]{1,0:T(8,128)(2,1)} async-done(((bf16[128,2048]{1,0:T(8,128)(2,1)}), bf16[2048,2048]{1,0:T(8,128)(2,1)}) %all-gather.27.cloned.1.call-update) | async-done | bytes 8388624 | tf_op jit(solution)/shard_map/all_gather | solution.py:136
  565.1 64.5 %all-gather.31.cloned.1.call-done = bf16[2048,2048]{1,0:T(8,128)(2,1)} async-done(((bf16[128,2048]{1,0:T(8,128)(2,1)}), bf16[2048,2048]{1,0:T(8,128)(2,1)}) %all-gather.31.cloned.1.call-update) | async-done | bytes 8388624 | tf_op jit(solution)/shard_map/all_gather | solution.py:141
  629.7 21.9 all-gather.29.cloned.1.call-done
  662.2 65.9 %all-gather.33.cloned.1.call-done = bf16[2048,2048]{1,0:T(8,128)(2,1)} async-done(((bf16[128,2048]{1,0:T(8,128)(2,1)}), bf16[2048,2048]{1,0:T(8,128)(2,1)}) %all-gather.33.cloned.1.call-update) | async-done | bytes 8388624 | tf_op jit(solution)/shard_map/all_gather | solution.py:142
  738.0 28.2 %reduce-scatter.14.cloned.1.call-done = f32[128,2048]{1,0:T(8,128)} async-done(((f32[256,2048]{1,0:T(8,128)}), f32[128,2048]{1,0:T(8,128)}) %reduce-scatter.14.cloned.1.call-update) | async-done | bytes 1048592 | tf_op jit(solution)/shard_map/reduce_scatter | solution.py:99
  769.4 39.5 %all-reduce.4 = (f32[]{:T(128)}, f32[]{:T(128)}) all-reduce(f32[]{:T(128)} %get-tuple-element.39, f32[]{:T(128)} %get-tuple-element.37), channel_id=1, replica_groups=mesh['dp'=16,'mp'=2] {'dp','mp'}, use_global_device_ids=true, to_apply=%region_14.15 | all-reduce | flops 2 | bytes 16 | tf_op jit(solution)/shard_map/psum | solution.py:240
  812.1 22.3 all-gather.35.cloned.1.call-done
  850.7 31.8 %reduce-scatter.16.cloned.1.call-done = f32[128,2048]{1,0:T(8,128)} async-done(((f32[256,2048]{1,0:T(8,128)}), f32[128,2048]{1,0:T(8,128)}) %reduce-scatter.16.cloned.1.call-update) | async-done | bytes 1048592 | tf_op jit(solution)/shard_map/reduce_scatter | solution.py:99
  937.0 313.7 %all-gather.39.cloned.1.call-done = f32[16,2,4,256,512]{4,3,2,1,0:T(8,128)} async-done(((f32[1,2,4,256,512]{4,3,2,1,0:T(8,128)}), f32[16,2,4,256,512]{4,3,2,1,0:T(8,128)}) %all-gather.39.cloned.1.call-update) | async-done | bytes 67108880 | tf_op jit(solution)/shard_map/all_gather | solution.py:16
  1250.7 23.4 reduce_sum.221
  1366.1 65.2 %all-reduce.5 = (f32[2048]{0:T(1024)S(1)}, f32[2048]{0:T(1024)S(1)}, f32[2048]{0:T(1024)S(1)}, f32[2048]{0:T(1024)S(1)}) all-reduce(f32[2048]{0:T(1024)S(1)} %get-tuple-element.18, f32[2048]{0:T(1024)S(1)} %get-tuple-element.23, f32[2048]{0:T(1024)S(1)} %copy-done.50, ...), channel_id=6, replica_groups=mesh['dp'=16,'mp'=2] {'dp'}, use_global_device_ids=true, to_apply=%region_28.29.clone | all-reduce | flops 8192 | bytes 65536
  1438.5 71.9 %reduce-scatter.30.cloned.1.call-done = f32[128,2048]{1,0:T(8,128)} async-done(((f32[2048,2048]{1,0:T(8,128)}), f32[128,2048]{1,0:T(8,128)}) %reduce-scatter.30.cloned.1.call-update) | async-done | bytes 1048592 | tf_op jit(solution)/shard_map/reduce_scatter | solution.py:258
  1510.4 181.2 %reduce-scatter.32.cloned.1.call-done = f32[128,2048]{1,0:T(8,128)} async-done(((f32[2048,2048]{1,0:T(8,128)}), f32[128,2048]{1,0:T(8,128)}) %reduce-scatter.32.cloned.1.call-update) | async-done | bytes 1048592 | tf_op jit(solution)/shard_map/reduce_scatter | solution.py:259
  1691.6 181.0 %reduce-scatter.28.cloned.1.call-done = f32[128,2048]{1,0:T(8,128)} async-done(((f32[2048,2048]{1,0:T(8,128)}), f32[128,2048]{1,0:T(8,128)}) %reduce-scatter.28.cloned.1.call-update) | async-done | bytes 1048592 | tf_op jit(solution)/shard_map/reduce_scatter | solution.py:334
  1872.6 181.1 %reduce-scatter.26.cloned.1.call-done = f32[128,2048]{1,0:T(8,128)} async-done(((f32[2048,2048]{1,0:T(8,128)}), f32[128,2048]{1,0:T(8,128)}) %reduce-scatter.26.cloned.1.call-update) | async-done | bytes 1048592 | tf_op jit(solution)/shard_map/reduce_scatter | solution.py:333
  2053.7 107.2 %reduce-scatter.22.cloned.1.call-done = f32[128,1024]{1,0:T(8,128)} async-done(((f32[2048,1024]{1,0:T(8,128)}), f32[128,1024]{1,0:T(8,128)}) %reduce-scatter.22.cloned.1.call-update) | async-done | bytes 524304 | tf_op jit(solution)/shard_map/reduce_scatter | solution.py:331
  2160.9 107.8 %reduce-scatter.20.cloned.1.call-done = f32[128,1024]{1,0:T(8,128)} async-done(((f32[2048,1024]{1,0:T(8,128)}), f32[128,1024]{1,0:T(8,128)}) %reduce-scatter.20.cloned.1.call-update) | async-done | bytes 524304 | tf_op jit(solution)/shard_map/reduce_scatter | solution.py:330
  2268.7 181.6 %reduce-scatter.24.cloned.1.call-done = f32[128,2048]{1,0:T(8,128)} async-done(((f32[2048,2048]{1,0:T(8,128)}), f32[128,2048]{1,0:T(8,128)}) %reduce-scatter.24.cloned.1.call-update) | async-done | bytes 1048592 | tf_op jit(solution)/shard_map/reduce_scatter | solution.py:332
  (306 shorter events, 328.6 us)
Async XLA Ops:
  7.2 65.6 %all-gather.17.cloned.1.call-start = ((), (), s32[]{:S(2)}) async-start(), calls=%async_computation.11 | async-start | bytes 1572864 | tf_op jit(solution)/shard_map/all_gather | solution.py:95
  53.1 72.4 %all-gather.25.cloned.1.call-start = ((), (), s32[]{:S(2)}) async-start(), calls=%async_computation.15 | async-start | bytes 4456448 | tf_op jit(solution)/shard_map/all_gather | solution.py:133
  53.8 122.7 %all-gather.23.cloned.1.call-start = ((), (), s32[]{:S(2)}) async-start(), calls=%async_computation.14 | async-start | bytes 4456448 | tf_op jit(solution)/shard_map/all_gather | solution.py:132
  54.5 196.9 %all-gather.21.cloned.1.call-start = ((), (), s32[]{:S(2)}) async-start(), calls=%async_computation.13 | async-start | bytes 8912896 | tf_op jit(solution)/shard_map/all_gather | solution.py:134
  55.1 271.2 %all-gather.19.cloned.1.call-start = ((), (), s32[]{:S(2)}) async-start(), calls=%async_computation.12 | async-start | bytes 8912896 | tf_op jit(solution)/shard_map/all_gather | solution.py:135
  55.7 384.0 %all-reduce.9.cloned.1.call-start = ((), (), s32[]{:S(2)}) async-start(), calls=%async_computation.16 | async-start | bytes 8388608 | tf_op jit(solution)/shard_map/psum | solution.py:214
  261.1 254.2 %all-gather.27.cloned.1.call-start = ((), (), s32[]{:S(2)}) async-start(), calls=%async_computation.17 | async-start | bytes 8912896 | tf_op jit(solution)/shard_map/all_gather | solution.py:136
  261.8 298.6 %reduce-scatter.12.cloned.1.call-start = ((), (), s32[]{:S(2)}) async-start(), calls=%async_computation.18 | async-start | bytes 3145728 | tf_op jit(solution)/shard_map/reduce_scatter | solution.py:99
  522.5 107.2 %all-gather.31.cloned.1.call-start = ((), (), s32[]{:S(2)}) async-start(), calls=%async_computation.20 | async-start | bytes 8912896 | tf_op jit(solution)/shard_map/all_gather | solution.py:141
  523.3 128.3 %all-gather.29.cloned.1.call-start = ((), (), s32[]{:S(2)}) async-start(), calls=%async_computation.19 | async-start | bytes 1572864 | tf_op jit(solution)/shard_map/all_gather | solution.py:95
  563.8 164.2 %all-gather.33.cloned.1.call-start = ((), (), s32[]{:S(2)}) async-start(), calls=%async_computation.21 | async-start | bytes 8912896 | tf_op jit(solution)/shard_map/all_gather | solution.py:142
  564.6 201.6 %reduce-scatter.14.cloned.1.call-start = ((), (), s32[]{:S(2)}) async-start(), calls=%async_computation.22 | async-start | bytes 3145728 | tf_op jit(solution)/shard_map/reduce_scatter | solution.py:99
  735.6 98.8 %all-gather.35.cloned.1.call-start = ((), (), s32[]{:S(2)}) async-start(), calls=%async_computation.23 | async-start | bytes 1572864 | tf_op jit(solution)/shard_map/all_gather | solution.py:95
  812.0 70.6 %reduce-scatter.16.cloned.1.call-start = ((), (), s32[]{:S(2)}) async-start(), calls=%async_computation.24 | async-start | bytes 3145728 | tf_op jit(solution)/shard_map/reduce_scatter | solution.py:99
  850.5 59.0 %all-gather.37.cloned.1.call-start = ((), (), s32[]{:S(2)}) async-start(), calls=%async_computation.25 | async-start | bytes 1572864 | tf_op jit(solution)/shard_map/all_gather | solution.py:95
  888.1 362.6 %all-gather.39.cloned.1.call-start = ((), (), s32[]{:S(2)}) async-start(), calls=%async_computation.26 | async-start | bytes 71303168 | tf_op jit(solution)/shard_map/all_gather | solution.py:16
  924.4 439.8 %reduce-scatter.18.cloned.1.call-start = ((), (), s32[]{:S(2)}) async-start(), calls=%async_computation.27 | async-start | bytes 3145728 | tf_op jit(solution)/shard_map/reduce_scatter | solution.py:99
  1295.8 214.6 %reduce-scatter.30.cloned.1.call-start = ((), (), s32[]{:S(2)}) async-start(), calls=%async_computation.33 | async-start | bytes 17825792 | tf_op jit(solution)/shard_map/reduce_scatter | solution.py:258
  1306.9 384.7 %reduce-scatter.32.cloned.1.call-start = ((), (), s32[]{:S(2)}) async-start(), calls=%async_computation.34 | async-start | bytes 17825792 | tf_op jit(solution)/shard_map/reduce_scatter | solution.py:259
  1317.5 555.1 %reduce-scatter.28.cloned.1.call-start = ((), (), s32[]{:S(2)}) async-start(), calls=%async_computation.32 | async-start | bytes 17825792 | tf_op jit(solution)/shard_map/reduce_scatter | solution.py:334
  1328.1 725.6 %reduce-scatter.26.cloned.1.call-start = ((), (), s32[]{:S(2)}) async-start(), calls=%async_computation.31 | async-start | bytes 17825792 | tf_op jit(solution)/shard_map/reduce_scatter | solution.py:333
  1337.6 823.3 %reduce-scatter.22.cloned.1.call-start = ((), (), s32[]{:S(2)}) async-start(), calls=%async_computation.29 | async-start | bytes 8912896 | tf_op jit(solution)/shard_map/reduce_scatter | solution.py:331
  1343.4 925.3 %reduce-scatter.20.cloned.1.call-start = ((), (), s32[]{:S(2)}) async-start(), calls=%async_computation.28 | async-start | bytes 8912896 | tf_op jit(solution)/shard_map/reduce_scatter | solution.py:330
  1349.3 1100.9 %reduce-scatter.24.cloned.1.call-start = ((), (), s32[]{:S(2)}) async-start(), calls=%async_computation.30 | async-start | bytes 17825792 | tf_op jit(solution)/shard_map/reduce_scatter | solution.py:332
  (72 other events, 2113.5 us)
Sparse Core Ops, SparseCore 0:
  53.2 19.6 all-gather.16
  75.0 50.3 all-gather.24
  127.6 48.8 all-gather.22
  178.5 72.8 all-gather.20
  253.4 72.8 all-gather.18
  329.9 109.7 all-reduce.8
  441.8 73.4 all-gather.26
  522.6 30.4 reduce-scatter.11
  555.3 74.3 all-gather.30
  631.6 19.8 all-gather.28
  653.7 74.2 all-gather.32
  735.7 30.4 reduce-scatter.13
  812.1 22.1 all-gather.34
  850.6 31.8 reduce-scatter.15
  888.2 21.2 all-gather.36
  924.5 326.0 all-gather.38
  1295.9 31.8 reduce-scatter.17
  1332.4 178.0 reduce-scatter.29
  1515.1 176.4 reduce-scatter.31
  1696.1 176.4 reduce-scatter.27
  1877.3 176.4 reduce-scatter.25
  2058.4 102.5 reduce-scatter.21
  2165.6 103.0 reduce-scatter.19
  2273.2 176.9 reduce-scatter.23
